TPU v7x, 32 devices: a whole 2x2x4 slice. The times are simulated.
32 devices in a mesh: groups: 2 (over x), blk: 16 (over z, y, core).
Axes of the slice: x: 2, y: 2, z: 4, core: 2. Of those that a mesh axis runs over, the one named last changes fastest.
Arguments:
- text_queries: bfloat16 [4096, 4096], P(('groups', 'blk')), parts along dimension 0, may hold values from -170 to 170
- image_states: bfloat16 [1536, 8192], P(('groups', 'blk')), parts along dimension 0, may hold values from -6 to 6
- kv_weight: bfloat16 [8192, 1024], P('blk'), may hold values from -0.1875 to 0.1875
- q_gain: float32 [128], replicated, may hold values from 0.25 to 1.75
- k_gain: float32 [128], replicated, may hold values from 0.25 to 1.75
- text_counts: int32 [6], P('groups'), parts along dimension 0, may hold values from 1 to 1024, 2048 in all
- image_counts: int32 [6], P('groups'), parts along dimension 0, may hold values from 96 to 384, as said below
Outputs:
- attended: bfloat16 [4096, 4096], P(('groups', 'blk')), parts along dimension 0
There are 2 independent parts, one for each index of `groups`. A program takes and returns all parts, laid end to end along the dimension named above; an argument that names none is the same for every part. Nothing has to cross between parts.
Inputs may be any that keep to these rules, and one draw needn't show every extreme that they name: `text_counts`: they sum to 2048. `image_counts`: they sum to 768; the second image has exactly 384 tokens, the first and last are cut by the window.
All inputs are finite; a program needn't handle non-finite values.
Results may differ from a plain program's by a relative error of at most 0.0071.
Values may be sent and summed in bfloat16 or wider, within the bound.
No kernel may reach another device: no remote copies, remote signals or barrier semaphores. Data moves between devices by JAX's collectives and lax.ppermute only.
A program may use at most 128 MiB of HBM per device.

v0:
```python
import math
import jax
import jax.numpy as jnp
from jax import lax
from jax.sharding import PartitionSpec as P

epsilon = 1e-05


def rms_norm(inputs, norm_gain):
    return (
        inputs * lax.rsqrt(jnp.mean(inputs * inputs, axis=-1, keepdims=True) + epsilon) * norm_gain
    )


def body(text_queries, image_states, kv_weight, q_gain, k_gain, text_counts, image_counts):
    head_dim = q_gain.shape[0]
    text_rows = text_queries.shape[0]
    image_rows = image_states.shape[0]
    kv_width = kv_weight.shape[1] // 2
    kv_heads = kv_width // head_dim
    query_heads = text_queries.shape[1] // head_dim
    group_size = query_heads // kv_heads
    columns = lax.all_to_all(image_states, "blk", split_axis=1, concat_axis=0, tiled=True)
    projected = lax.psum_scatter(
        jnp.dot(columns, kv_weight, preferred_element_type=jnp.float32),
        "blk",
        scatter_dimension=0,
        tiled=True,
    )
    image_keys = rms_norm(projected[:, :kv_width].reshape(image_rows, kv_heads, head_dim), k_gain)
    image_keys = image_keys.astype(jnp.bfloat16).reshape(image_rows, kv_width)
    image_values = projected[:, kv_width:].astype(jnp.bfloat16)
    kv_rows_local = jnp.concatenate([image_keys, image_values], axis=1)
    normed_queries = rms_norm(
        text_queries.astype(jnp.float32).reshape(text_rows, query_heads, head_dim), q_gain
    )
    normed_queries = normed_queries.astype(jnp.bfloat16).reshape(
        text_rows, kv_heads, group_size, head_dim
    )
    text_positions = lax.axis_index("blk") * text_rows + jnp.arange(text_rows, dtype=jnp.int32)
    text_ends = jnp.cumsum(text_counts)
    image_ends = jnp.cumsum(image_counts)
    text_segment = jnp.sum(
        (text_ends[None, :] <= text_positions[:, None]).astype(jnp.int32), axis=1
    )
    score_scale = 1.0 / math.sqrt(head_dim)
    arrived = lax.all_gather(kv_rows_local, "blk", axis=0, tiled=True)
    first_row = jnp.int32(0)
    numerator = jnp.zeros((kv_heads, group_size, text_rows, head_dim), jnp.float32)
    denominator = jnp.zeros((kv_heads, group_size, text_rows), jnp.float32)
    key_span = arrived.shape[0]
    for offset in range(0, key_span, 512):
        block_size = min(512, key_span - offset)
        key_block = arrived[offset : offset + block_size]
        key_heads = key_block[:, :kv_width].reshape(block_size, kv_heads, head_dim)
        value_heads = key_block[:, kv_width:].reshape(block_size, kv_heads, head_dim)
        key_positions = first_row + offset + jnp.arange(block_size, dtype=jnp.int32)
        key_owner = jnp.sum(
            (image_ends[None, :] <= key_positions[:, None]).astype(jnp.int32), axis=1
        )
        allowed = key_owner[None, :] <= text_segment[:, None]
        scores = (
            jnp.einsum(
                "tgrd,pgd->grtp", normed_queries, key_heads, preferred_element_type=jnp.float32
            )
            * score_scale
        )
        weights = jnp.where(allowed, jnp.exp(scores), 0.0)
        denominator = denominator + jnp.sum(weights, axis=-1)
        numerator = numerator + jnp.einsum(
            "grtp,pgd->grtd",
            weights.astype(jnp.bfloat16),
            value_heads,
            preferred_element_type=jnp.float32,
        )
    numerator, denominator = (numerator, denominator)
    attended = (numerator / denominator[..., None]).astype(jnp.bfloat16)
    return jnp.transpose(attended, (2, 0, 1, 3)).reshape(text_rows, query_heads * head_dim)


def solution(mesh):
    placed = (
        P(("groups", "blk"), None),
        P(("groups", "blk"), None),
        P("blk", None),
        P(),
        P(),
        P("groups"),
        P("groups"),
    )
    return jax.shard_map(
        body, mesh=mesh, in_specs=placed, out_specs=P(("groups", "blk"), None), check_vma=False
    )
```

profile of v0, /device:TPU:0, one launch (start us, length us, event | category | flops | bytes accessed | tf_op | source)
XLA Modules:
  0.0 173.4 jit_solution(13814516155407754564)
XLA Ops:
  6.5 0.0 copy-start
  6.5 0.0 reduce-scatter.2.cloned.1.call-start
  6.5 1.3 copy.124
  7.8 27.3 %all_to_all.19 = bf16[48,16,512]{2,0,1:T(8,128)(2,1)S(1)} all-to-all(bf16[48,16,512]{2,0,1:T(8,128)(2,1)S(1)} %bitcast.70), channel_id=1, replica_groups=mesh['groups'=2,'blk'=16] {'blk'}, dimensions={1} | all-to-all | bytes 1572864 | tf_op jit(solution)/shard_map/all_to_all | solution.py:24
  35.2 0.0 copy-done
  35.2 2.6 %fusion.34 = f32[768,1024]{1,0:T(8,128)} fusion(bf16[768,512]{1,0:T(8,128)(2,1)S(1)} %bitcast.69, bf16[512,1024]{1,0:T(8,128)(2,1)S(1)} %copy-done), kind=kOutput, calls=%fused_computation.51 | convolution fusion | flops 805306368 | bytes 4980736 | tf_op jit(solution)/shard_map/dot_general | solution.py:26
  37.8 0.0 copy-start.4
  37.8 0.0 copy-start.5
  37.8 0.0 copy-start.6
  37.8 0.0 copy-start.1
  37.8 0.0 reduce-scatter.2.cloned.1.call-update
  37.9 0.0 all-gather.2.cloned.1.call-start
  37.9 0.6 copy-done.4
  38.5 65.1 %reduce-scatter.2.cloned.1.call-done = f32[48,1024]{1,0:T(8,128)} async-done(((f32[768,1024]{1,0:T(8,128)}), f32[48,1024]{1,0:T(8,128)}) %reduce-scatter.2.cloned.1.call-update) | async-done | bytes 196624 | tf_op jit(solution)/shard_map/reduce_scatter | solution.py:25
  103.6 0.9 slice_multiply_fusion
  104.5 0.1 reduce_sum.65
  104.7 0.9 slice.40
  105.6 0.1 mul.74
  105.7 0.9 fusion.27
  106.6 0.6 pad_maximum_fusion
  107.3 0.0 all-gather.2.cloned.1.call-update
  107.3 0.0 copy-done.5
  107.3 0.2 reduce-window.17
  107.5 0.0 copy-done.6
  107.5 0.2 reduce-window.16
  107.7 0.0 copy-done.1
  107.7 0.2 fusion.9
  107.9 0.4 copy.101
  108.3 0.6 reduce_sum.66
  108.9 0.1 copy.77
  108.9 1.4 convert_bitcast_fusion
  110.4 0.4 copy.100
  110.8 0.1 convert_reduce_fusion
  110.9 0.1 convert_reduce_fusion.2
  110.9 0.1 convert_reduce_fusion.1
  111.0 0.1 broadcast_compare_fusion.1
  111.2 0.1 broadcast_compare_fusion
  111.3 34.7 %all-gather.2.cloned.1.call-done = bf16[768,1024]{1,0:T(8,128)(2,1)} async-done(((bf16[48,1024]{1,0:T(8,128)(2,1)}), bf16[768,1024]{1,0:T(8,128)(2,1)}) %all-gather.2.cloned.1.call-update) | async-done | bytes 1572880 | tf_op jit(solution)/shard_map/all_gather | solution.py:48
  146.0 2.2 %fusion.32 = (bf16[512,512]{1,0:T(8,128)(2,1)}, bf16[512,512]{1,0:T(8,128)(2,1)}) fusion(bf16[768,1024]{1,0:T(8,128)(2,1)} %all-gather.2.cloned.1.call-done), kind=kLoop, calls=%fused_computation.49 | loop fusion | bytes 2097152 | tf_op jit(solution)/shard_map/slice | solution.py:56
  148.3 0.0 copy-start.7
  148.3 2.0 %reshape.123 = bf16[512,4,128]{2,1,0:T(4,128)(2,1)} reshape(bf16[512,512]{1,0:T(8,128)(2,1)} %get-tuple-element.5) | data formatting | bytes 1048576 | tf_op jit(solution)/shard_map/reshape | solution.py:56
  150.2 1.8 %fusion.33 = (bf16[256,512]{1,0:T(8,128)(2,1)S(1)}, bf16[256,512]{1,0:T(8,128)(2,1)}) fusion(bf16[768,1024]{1,0:T(8,128)(2,1)} %all-gather.2.cloned.1.call-done), kind=kLoop, calls=%fused_computation.50 | loop fusion | bytes 1048576 | tf_op jit(solution)/shard_map/slice | solution.py:56
  152.0 0.8 reshape.126
  152.8 1.1 copy.97
  153.9 2.0 %copy.94 = bf16[512,512]{0,1:T(8,128)(2,1)} copy(bf16[512,512]{1,0:T(8,128)(2,1)} %get-tuple-element.6) | data formatting | bytes 1048576 | tf_op jit(solution)/shard_map/reshape | solution.py:57
  155.9 0.0 copy-done.7
  155.9 3.2 %fusion.7 = (f32[4,8,128]{2,1,0:T(8,128)S(1)}, f32[4,256,128,8]{2,1,3,0:T(8,128)S(1)}) fusion(pred[128,256]{0,1:T(8,128)(4,1)S(1)} %broadcast_compare_fusion.1, f32[128,4,8,128]{3,2,1,0:T(8,128)S(1)} %bitcast.71, f32[128]{0:T(128)S(1)} %copy-done.7, f32[128,4,8]{0,2,1:T(8,128)S(1)} %rsqrt_bitcast_fusion, bf16[256,4,128,1]{2,1,0,3:T(4,128)(2,1)} %bitcast.79), kind=kOutput, calls=%fused_computation.8 | convolution fusion | flops 273149952 | bytes 6619648 | tf_op jit(solution)/shard_map/tgrd,pgd->grtp/dot_general | solution.py:64
  159.1 0.0 copy-start.2
  159.1 0.9 fusion.10
  160.0 0.2 copy-done.2
  160.2 0.0 copy-start.3
  160.2 3.3 %fusion = (f32[4,8,128]{2,1,0:T(8,128)S(1)}, f32[4,512,128,8]{2,1,3,0:T(8,128)S(1)}) fusion(pred[128,512]{0,1:T(8,128)(4,1)S(1)} %broadcast_compare_fusion, f32[128,4,8,128]{3,2,1,0:T(8,128)S(1)} %bitcast.72, f32[128]{0:T(128)S(1)} %copy-done.7, f32[128,4,8]{0,2,1:T(8,128)S(1)} %rsqrt_bitcast_fusion, bf16[512,4,128,1]{2,1,0,3:T(4,128)(2,1)S(1)} %bitcast.76), kind=kOutput, calls=%fused_computation.1 | convolution fusion | flops 544731136 | bytes 11108864 | tf_op jit(solution)/shard_map/tgrd,pgd->grtp/dot_general | solution.py:64
  163.5 0.0 copy-done.3
  163.5 1.8 %fusion.12 = bf16[128,4,8,128]{0,3,2,1:T(8,128)(2,1)S(1)} fusion(f32[4,8,128,128]{2,3,1,0:T(8,128)S(1)} %fusion.10, bf16[512,4,128,1]{0,2,3,1:T(8,128)(2,1)S(1)} %bitcast.77, f32[4,512,128,8]{2,1,3,0:T(8,128)S(1)} %get-tuple-element.10, pred[128,512]{0,1:T(8,128)(4,1)S(1)} %broadcast_compare_fusion, f32[128,4,8]{0,2,1:T(8,128)S(1)} %add_bitcast_fusion), kind=kOutput, calls=%fused_computation.15 | convolution fusion | flops 544735232 | bytes 12140544 | tf_op jit(solution)/shard_map/grtp,pgd->grtd/dot_general | solution.py:71
  165.3 1.3 copy.85
  (7 shorter events, 0.1 us)
Async XLA Ops:
  6.5 28.6 %copy-start = (bf16[512,1024]{1,0:T(8,128)(2,1)S(1)}, bf16[512,1024]{1,0:T(8,128)(2,1)}, u32[]{:S(2)}) copy-start(bf16[512,1024]{1,0:T(8,128)(2,1)} %param.9) | copy-start | bytes 3145732
  6.5 97.0 %reduce-scatter.2.cloned.1.call-start = ((), (), s32[]{:S(2)}) async-start(), calls=%async_computation.2 | async-start | bytes 3342336 | tf_op jit(solution)/shard_map/reduce_scatter | solution.py:25
  37.8 0.7 copy-start.4
  37.8 69.5 %copy-start.5 = (s32[3]{0:T(128)S(1)}, s32[3]{0:T(128)}, u32[]{:S(2)}) copy-start(s32[3]{0:T(128)} %param.12) | copy-start | bytes 40
  37.8 69.6 %copy-start.6 = (s32[3]{0:T(128)S(1)}, s32[3]{0:T(128)}, u32[]{:S(2)}) copy-start(s32[3]{0:T(128)} %param.13) | copy-start | bytes 40
  37.8 69.8 %copy-start.1 = (bf16[128,4096]{1,0:T(8,128)(2,1)S(1)}, bf16[128,4096]{1,0:T(8,128)(2,1)}, u32[]{:S(2)}) copy-start(bf16[128,4096]{1,0:T(8,128)(2,1)} %param.7) | copy-start | bytes 3145732
  37.9 108.2 %all-gather.2.cloned.1.call-start = ((), (), s32[]{:S(2)}) async-start(), calls=%async_computation.3 | async-start | bytes 1671168 | tf_op jit(solution)/shard_map/all_gather | solution.py:48
  148.3 7.7 %copy-start.7 = (f32[128]{0:T(128)S(1)}, f32[128]{0:T(128)}, u32[]{:S(2)}) copy-start(f32[128]{0:T(128)} %param.10) | copy-start | bytes 1540
  159.1 1.0 copy-start.2
  160.2 3.3 %copy-start.3 = (bf16[512,512]{0,1:T(8,128)(2,1)S(1)}, bf16[512,512]{0,1:T(8,128)(2,1)}, u32[]{:S(2)}) copy-start(bf16[512,512]{0,1:T(8,128)(2,1)} %copy.94) | copy-start | bytes 1572868
Sparse Core Ops, SparseCore 0:
  38.0 65.5 reduce-scatter.1
  107.4 38.5 all-gather.1
where the time goes:
time: 174 us; the launch traced here: 173 us
  waiting for transfers between devices  99.9 us (57%)
  blocking collectives  27.3 us (16%)
  local copies, waits for them, and re-layouts  15.1 us (9%)
  between operations  13.6 us (8%)
  matrix products  11.8 us (7%)
  other arithmetic  5.74 us (3%)
    reduce_scatter x1, waiting for transfers between devices, body(): lax.psum_scatter(jnp.dot(columns, kv_weight, preferred_element_type=jnp.f...  65.1 us
    all_gather x1, waiting for transfers between devices, body(): arrived = lax.all_gather(kv_rows_local, 'blk', axis=0, tiled=True)  34.7 us
    all_to_all x1, blocking collectives, body(): lax.all_to_all(image_states, 'blk', split_axis=1, concat_axis=0, tiled=True)  27.3 us
    dot_general x2, matrix products, body(): jnp.einsum('tgrd,pgd->grtp', normed_queries, key_heads, preferred_element...  6.52 us
    slice x2, local copies, waits for them, and re-layouts, body(): key_heads = key_block[:, :kv_width].reshape(block_size, kv_heads, head_dim)  4 us
  transfers between devices with their start and end apart: 2, of which 2 were waited for; matrix products, arithmetic and copies ran while one was open for 2% of the time, Pallas kernels for 0%

commit v1 on v0

--- a/solution.py
+++ b/solution.py
@@ -5,6 +5,18 @@
 from jax.sharding import PartitionSpec as P
 
 epsilon = 1e-05
+
+
+def doubled_up(shard, axis, dim):
+    ways, here = (lax.axis_size(axis), lax.axis_index(axis))
+    grown, reach = (shard, 1)
+    while reach < ways:
+        theirs = lax.ppermute(grown, axis, [(d, d ^ reach) for d in range(ways)])
+        mine_first = jnp.concatenate([grown, theirs], axis=dim)
+        theirs_first = jnp.concatenate([theirs, grown], axis=dim)
+        grown = jnp.where(here & reach == 0, mine_first, theirs_first)
+        reach = 2 * reach
+    return grown
 
 
 def rms_norm(inputs, norm_gain):
@@ -45,7 +57,7 @@
         (text_ends[None, :] <= text_positions[:, None]).astype(jnp.int32), axis=1
     )
     score_scale = 1.0 / math.sqrt(head_dim)
-    arrived = lax.all_gather(kv_rows_local, "blk", axis=0, tiled=True)
+    arrived = doubled_up(kv_rows_local, "blk", 0)
     first_row = jnp.int32(0)
     numerator = jnp.zeros((kv_heads, group_size, text_rows, head_dim), jnp.float32)
     denominator = jnp.zeros((kv_heads, group_size, text_rows), jnp.float32)

time: 174 us -> 191 us (1.098)
  other arithmetic: 5.74 us -> 13.9 us
  starting transfers between devices: 0.04 us -> 3.92 us
  waiting for transfers between devices: 99.9 us -> 103 us
    ppermute x0 -> x4, waiting for transfers between devices: none -> 38.3 us  [doubled_up(): theirs = lax.ppermute(grown, axis, [(d, d ^ reach) for d in range(ways)])]
    all_gather x1 -> x0, waiting for transfers between devices: 34.7 us -> none  [body(): arrived = lax.all_gather(kv_rows_local, 'blk', axis=0, tiled=True)]
    ppermute x0 -> x4, starting transfers between devices: none -> 3.92 us  [doubled_up(): theirs = lax.ppermute(grown, axis, [(d, d ^ reach) for d in range(ways)])]
    unnamed x18 -> x26, local copies, waits for them, and re-layouts: 1.5 us -> 4.22 us
    unnamed x2, other arithmetic: 1.66 us -> 4.23 us
    reduce_sum x2, other arithmetic: 0.73 us -> 3.11 us  [rms_norm(): jnp.mean(inputs * inputs, axis=-1, keepdims=True) + epsilon]
    select_n x0 -> x4, other arithmetic: none -> 2.24 us  [doubled_up(): grown = jnp.where(here & reach == 0, mine_first, theirs_first)]
    slice x2, local copies, waits for them, and re-layouts: 4 us -> 1.81 us  [body(): key_heads = key_block[:, :kv_width].reshape(block_size, kv_heads, head_dim)]
  transfers between devices with their start and end apart: 2 -> 5, of which waited for: 2 -> 4; matrix products, arithmetic and copies ran while one was open for 2% -> 7% of each run, Pallas kernels for 0% -> 0%
where the time goes in v1:
time: 191 us
  waiting for transfers between devices  103 us (54%)
  blocking collectives  27.3 us (14%)
  local copies, waits for them, and re-layouts  16.6 us (9%)
  other arithmetic  13.9 us (7%)
  between operations  13.6 us (7%)
  matrix products  11.8 us (6%)
  starting transfers between devices  3.92 us (2%)
    reduce_scatter x1, waiting for transfers between devices, body(): lax.psum_scatter(jnp.dot(columns, kv_weight, preferred_element_type=jnp.f...  65.1 us
    ppermute x4, waiting for transfers between devices, doubled_up(): theirs = lax.ppermute(grown, axis, [(d, d ^ reach) for d in range(ways)])  38.3 us
    all_to_all x1, blocking collectives, body(): lax.all_to_all(image_states, 'blk', split_axis=1, concat_axis=0, tiled=True)  27.3 us
    dot_general x2, matrix products, body(): jnp.einsum('tgrd,pgd->grtp', normed_queries, key_heads, preferred_element...  6.52 us
    unnamed x2, other arithmetic  4.23 us
    unnamed x26, local copies, waits for them, and re-layouts  4.22 us
    ppermute x4, starting transfers between devices, doubled_up(): theirs = lax.ppermute(grown, axis, [(d, d ^ reach) for d in range(ways)])  3.92 us
  transfers between devices with their start and end apart: 5, of which 4 were waited for; matrix products, arithmetic and copies ran while one was open for 7% of the time, Pallas kernels for 0%

profile of v1, /device:TPU:0, one launch (start us, length us, event | category | flops | bytes accessed | tf_op | source)
XLA Modules:
  0.0 190.5 jit_solution(7807019636808100631)
XLA Ops:
  6.5 0.0 copy-start
  6.5 0.0 reduce-scatter.2.cloned.1.call-start
  6.5 1.3 copy.124
  7.8 27.3 %all_to_all.19 = bf16[48,16,512]{2,0,1:T(8,128)(2,1)S(1)} all-to-all(bf16[48,16,512]{2,0,1:T(8,128)(2,1)S(1)} %bitcast.70), channel_id=1, replica_groups=mesh['groups'=2,'blk'=16] {'blk'}, dimensions={1} | all-to-all | bytes 1572864 | tf_op jit(solution)/shard_map/all_to_all | solution.py:36
  35.2 0.0 copy-done
  35.2 2.6 %fusion.34 = f32[768,1024]{1,0:T(8,128)} fusion(bf16[768,512]{1,0:T(8,128)(2,1)S(1)} %bitcast.69, bf16[512,1024]{1,0:T(8,128)(2,1)S(1)} %copy-done), kind=kOutput, calls=%fused_computation.55 | convolution fusion | flops 805306368 | bytes 4980736 | tf_op jit(solution)/shard_map/dot_general | solution.py:38
  37.8 0.0 reduce-scatter.2.cloned.1.call-update
  37.9 0.6 copy-done.6
  38.5 65.1 %reduce-scatter.2.cloned.1.call-done = f32[48,1024]{1,0:T(8,128)} async-done(((f32[768,1024]{1,0:T(8,128)}), f32[48,1024]{1,0:T(8,128)}) %reduce-scatter.2.cloned.1.call-update) | async-done | bytes 196624 | tf_op jit(solution)/shard_map/reduce_scatter | solution.py:37
  103.6 0.9 slice_multiply_fusion
  104.5 0.1 reduce_sum.65
  104.7 0.9 slice.40
  105.6 0.1 mul.74
  105.7 0.9 fusion.27
  106.6 0.1 collective-permute-start
  106.7 1.4 fusion.9
  108.2 0.0 copy-start.7
  108.2 0.0 copy-start.8
  108.2 0.0 collective-permute-done
  108.2 1.0 collective-permute-start.1
  109.3 2.8 %convert_bitcast_fusion = f32[16,8,32,128]{3,1,2,0:T(8,128)} fusion(bf16[128,4096]{1,0:T(8,128)(2,1)} %param.7), kind=kLoop, calls=%fused_computation.11 | loop fusion | flops 524288 | bytes 3145728
  112.1 3.5 %collective-permute-done.1 = bf16[96,1024]{1,0:T(8,128)(2,1)S(1)} collective-permute-done((bf16[96,1024]{1,0:T(8,128)(2,1)S(1)}, bf16[96,1024]{1,0:T(8,128)(2,1)S(1)}, u32[]{:S(2)}, u32[]{:S(2)}) %collective-permute-start.1) | collective-permute-done | bytes 196640 | tf_op jit(solution)/shard_map/ppermute | solution.py:14
  115.6 0.1 maximum_select_fusion.2
  115.7 1.3 collective-permute-start.2
  117.0 0.5 iota_add_fusion.1
  117.5 0.0 copy-done.7
  117.5 0.7 reduce-window.17
  118.2 0.0 copy-done.8
  118.2 0.7 reduce-window.16
  118.9 1.7 copy.101
  120.6 3.0 %reduce_sum.66 = f32[128,32]{1,0:T(8,128)} reduce(f32[128,32,128]{2,1,0:T(8,128)} %bitcast.68, f32[]{:T(128)} %constant.8.clone.1), dimensions={2}, to_apply=%region_6.7 | reduce | flops 520192 | bytes 2113540 | tf_op jit(solution)/shard_map/reduce_sum | solution.py:24
  123.6 0.9 copy.77
  124.4 0.0 copy-done.1
  124.5 0.0 copy-start.11
  124.5 0.0 copy-start.5
  124.5 1.7 copy.100
  126.2 0.0 copy-done.10
  126.2 0.0 copy-done.11
  126.2 0.1 convert_reduce_fusion.2
  126.3 0.0 copy-done.5
  126.3 0.1 convert_reduce_fusion.1
  126.4 0.1 collective-permute-done.2
  126.5 1.4 maximum_select_fusion.1
  128.0 1.5 collective-permute-start.3
  129.5 0.1 convert_reduce_fusion
  129.6 0.1 broadcast_compare_fusion.1
  129.7 0.1 broadcast_compare_fusion
  129.8 34.6 %collective-permute-done.3 = bf16[384,1024]{1,0:T(8,128)(2,1)S(1)} collective-permute-done((bf16[384,1024]{1,0:T(8,128)(2,1)S(1)}, bf16[384,1024]{1,0:T(8,128)(2,1)S(1)}, u32[]{:S(2)}, u32[]{:S(2)}) %collective-permute-start.3) | collective-permute-done | bytes 786464 | tf_op jit(solution)/shard_map/ppermute | solution.py:14
  164.5 0.7 maximum_select_fusion
  165.2 0.8 fusion.33
  165.9 1.1 fusion.32
  167.0 2.1 %reshape.123 = bf16[512,4,128]{2,1,0:T(4,128)(2,1)} reshape(bf16[512,512]{1,0:T(8,128)(2,1)} %get-tuple-element.5) | data formatting | bytes 1048576 | tf_op jit(solution)/shard_map/reshape | solution.py:68
  169.1 0.8 reshape.126
  169.9 1.1 copy.97
  170.9 2.0 %copy.94 = bf16[512,512]{0,1:T(8,128)(2,1)} copy(bf16[512,512]{1,0:T(8,128)(2,1)} %get-tuple-element.6) | data formatting | bytes 1048576 | tf_op jit(solution)/shard_map/reshape | solution.py:69
  173.0 0.0 copy-done.2
  173.0 0.0 copy-done.9
  173.0 3.2 %fusion.7 = (f32[4,8,128]{2,1,0:T(8,128)S(1)}, f32[4,256,128,8]{2,1,3,0:T(8,128)S(1)}) fusion(pred[128,256]{0,1:T(8,128)(4,1)S(1)} %broadcast_compare_fusion.1, f32[128,4,8,128]{3,2,1,0:T(8,128)S(1)} %bitcast.71, f32[128]{0:T(128)S(1)} %copy-done.9, f32[128,4,8]{0,2,1:T(8,128)S(1)} %rsqrt_bitcast_fusion, bf16[256,4,128,1]{2,1,0,3:T(4,128)(2,1)} %bitcast.79), kind=kOutput, calls=%fused_computation.8 | convolution fusion | flops 273149952 | bytes 6619648 | tf_op jit(solution)/shard_map/tgrd,pgd->grtp/dot_general | solution.py:76
  176.2 0.0 copy-start.3
  176.2 0.9 fusion.10
  177.1 0.2 copy-done.3
  177.3 3.3 %fusion = (f32[4,8,128]{2,1,0:T(8,128)S(1)}, f32[4,512,128,8]{2,1,3,0:T(8,128)S(1)}) fusion(pred[128,512]{0,1:T(8,128)(4,1)S(1)} %broadcast_compare_fusion, f32[128,4,8,128]{3,2,1,0:T(8,128)S(1)} %bitcast.72, f32[128]{0:T(128)S(1)} %copy-done.9, f32[128,4,8]{0,2,1:T(8,128)S(1)} %rsqrt_bitcast_fusion, bf16[512,4,128,1]{2,1,0,3:T(4,128)(2,1)S(1)} %bitcast.76), kind=kOutput, calls=%fused_computation.1 | convolution fusion | flops 544731136 | bytes 11108864 | tf_op jit(solution)/shard_map/tgrd,pgd->grtp/dot_general | solution.py:76
  180.6 1.8 fusion.12
  182.3 1.3 copy.85
  (15 shorter events, 0.1 us)
Async XLA Ops:
  6.5 28.6 %copy-start = (bf16[512,1024]{1,0:T(8,128)(2,1)S(1)}, bf16[512,1024]{1,0:T(8,128)(2,1)}, u32[]{:S(2)}) copy-start(bf16[512,1024]{1,0:T(8,128)(2,1)} %param.9) | copy-start | bytes 3145732
  6.5 97.0 %reduce-scatter.2.cloned.1.call-start = ((), (), s32[]{:S(2)}) async-start(), calls=%async_computation.2 | async-start | bytes 3342336 | tf_op jit(solution)/shard_map/reduce_scatter | solution.py:37
  37.8 0.7 copy-start.6
  106.6 1.6 collective-permute-start
  108.2 9.3 %copy-start.7 = (s32[3]{0:T(128)S(1)}, s32[3]{0:T(128)}, u32[]{:S(2)}) copy-start(s32[3]{0:T(128)} %param.12) | copy-start | bytes 40
  108.2 10.0 %copy-start.8 = (s32[3]{0:T(128)S(1)}, s32[3]{0:T(128)}, u32[]{:S(2)}) copy-start(s32[3]{0:T(128)} %param.13) | copy-start | bytes 40
  108.2 7.4 %collective-permute-start.1 = (bf16[96,1024]{1,0:T(8,128)(2,1)S(1)}, bf16[96,1024]{1,0:T(8,128)(2,1)S(1)}, u32[]{:S(2)}, u32[]{:S(2)}) collective-permute-start(bf16[96,1024]{1,0:T(8,128)(2,1)S(1)} %maximum_select_fusion.3), channel_id=1, source_target_pairs={{0,2},{1,3},{2,0},{3,1},{4,6},{5,7},{6,4},{7,5},{8,10},{9,11},{10,... | collective-permute-start | bytes 589832 | tf_op jit(solution)/shard_map/ppermute | solution.py:14
  115.7 10.8 %collective-permute-start.2 = (bf16[192,1024]{1,0:T(8,128)(2,1)S(1)}, bf16[192,1024]{1,0:T(8,128)(2,1)}, u32[]{:S(2)}, u32[]{:S(2)}) collective-permute-start(bf16[192,1024]{1,0:T(8,128)(2,1)S(1)} %maximum_select_fusion.2), channel_id=1, source_target_pairs={{0,4},{1,5},{2,6},{3,7},{4,0},{5,1},{6,2},{7,3},{8,12},{9,13},{10,... | collective-permute-start | bytes 1179656 | tf_op jit(solution)/shard_map/ppermute | solution.py:14
  120.6 3.9 %copy-start.1 = (f32[16,8,32,128]{3,1,2,0:T(8,128)S(1)}, f32[16,8,32,128]{3,1,2,0:T(8,128)}, u32[]{:S(2)}) copy-start(f32[16,8,32,128]{3,1,2,0:T(8,128)} %convert_bitcast_fusion) | copy-start | bytes 6291460
  124.4 1.8 copy-start.10
  124.5 1.7 copy-start.11
  124.5 1.8 copy-start.5
  128.0 36.5 %collective-permute-start.3 = (bf16[384,1024]{1,0:T(8,128)(2,1)S(1)}, bf16[384,1024]{1,0:T(8,128)(2,1)S(1)}, u32[]{:S(2)}, u32[]{:S(2)}) collective-permute-start(bf16[384,1024]{1,0:T(8,128)(2,1)S(1)} %maximum_select_fusion.1), channel_id=1, source_target_pairs={{0,8},{1,9},{2,10},{3,11},{4,12},{5,13},{6,14},{7,15},{8,0},{9,1},... | collective-permute-start | bytes 2359304 | tf_op jit(solution)/shard_map/ppermute | solution.py:14
  167.0 6.0 %copy-start.2 = (f32[16,8,32,128]{3,2,1,0:T(8,128)S(1)}, f32[16,8,32,128]{3,2,1,0:T(8,128)}, u32[]{:S(2)}) copy-start(f32[16,8,32,128]{3,2,1,0:T(8,128)} %copy.100) | copy-start | bytes 6291460
  167.0 6.0 %copy-start.9 = (f32[128]{0:T(128)S(1)}, f32[128]{0:T(128)}, u32[]{:S(2)}) copy-start(f32[128]{0:T(128)} %param.10) | copy-start | bytes 1540
  176.2 1.0 copy-start.3
  177.3 3.3 %copy-start.4 = (bf16[512,512]{0,1:T(8,128)(2,1)S(1)}, bf16[512,512]{0,1:T(8,128)(2,1)}, u32[]{:S(2)}) copy-start(bf16[512,512]{0,1:T(8,128)(2,1)} %copy.94) | copy-start | bytes 1572868
Sparse Core Ops, SparseCore 0:
  38.0 65.5 reduce-scatter.1
